TPU v7x, 512 devices: a whole 4x8x8 slice. The times are simulated.
512 devices in a mesh: cells: 128 (over z, y, core), slab: 4 (over x).
Axes of the slice: x: 4, y: 8, z: 8, core: 2. Of those that a mesh axis runs over, the one named last changes fastest.
Arguments:
- centres: float32 [4, 512, 3, 1024], P('slab', 'cells'), may hold values from -6 to 6
- tangents: float32 [4, 512, 3, 1024], P('slab', 'cells'), may hold values from -3.5 to 3.5
- weights: float32 [4, 512, 1024], P('slab', 'cells'), may hold values from -2 to 2
- segment_count: int32 [4, 512], P('slab', 'cells'), may hold values from 512 to 1024
- pairs: int32 [4, 1280, 2], P('slab', 'cells'), may hold values from 0 to 1023, as said below
- pair_count: int32 [4, 128], P('slab', 'cells'), may hold values from 3 to 10, as said below
Outputs:
- grad_centres: float32 [4, 512, 3, 1024], P('slab', 'cells')
- grad_tangents: float32 [4, 512, 3, 1024], P('slab', 'cells')
Inputs may be any that keep to these rules, and one draw needn't show every extreme that they name: Slot entries (i, j) of device (s, c): i is a block owned by that device (c * 4 to c * 4 + 3); the block that j names lies within 2 blocks of i in the slab's order; j names the slab above only below the top slab. No unordered block pair is held by two live slots over all devices. Slots at or beyond pair_count also hold pairs that obey these rules. `pair_count`: some device has all 10 slots live.
All inputs are finite; a program needn't handle non-finite values.
Results may differ from a plain program's by a relative error of at most 0.0003.
Values sent between devices are 32-bit elements; how exact they have to be, the bound alone decides.
A program may use at most 64 MiB of HBM per device.

v0:
```python
import jax
import jax.numpy as jnp
from jax import lax
from jax.sharding import PartitionSpec as P

REACH = 2


width_square = 4.0


def from_behind(value, axis, by):
    peers = lax.axis_size(axis)
    pairs = [(i, i + by) for i in range(peers) if 0 <= i + by < peers]
    return lax.ppermute(value, axis, pairs)


def with_halo(block, sides, width):
    for axis, dim in sides:
        count = lax.axis_size(axis)
        forward = [(i, i + 1) for i in range(count - 1)]
        backward = [(target, source) for source, target in forward]
        low = lax.ppermute(
            lax.slice_in_dim(block, block.shape[dim] - width, None, axis=dim), axis, forward
        )
        high = lax.ppermute(lax.slice_in_dim(block, 0, width, axis=dim), axis, backward)
        block = jnp.concatenate([low, block, high], axis=dim)
    return block


def tile_terms(left_block, right_block, factor):
    highest = lax.Precision.HIGHEST
    segments = left_block.shape[1]
    row_block = min(512, segments)
    right_pos = right_block[0:3]
    right_dir = right_block[3:6]
    right_weight = right_block[6]
    right_grad = jnp.zeros((6, segments), jnp.float32)
    left_parts = []
    for row_start in range(0, segments, row_block):
        row_part = left_block[:, row_start : row_start + row_block]
        left_pos = row_part[0:3]
        left_dir = row_part[3:6]
        left_weight = row_part[6]
        distance = jnp.sum((left_pos[:, :, None] - right_pos[:, None, :]) ** 2, axis=0)
        gauss = jnp.exp(-distance / width_square)
        cosine = (
            left_dir[0][:, None] * right_dir[0][None, :]
            + left_dir[1][:, None] * right_dir[1][None, :]
            + left_dir[2][:, None] * right_dir[2][None, :]
        )
        first_order = left_weight[:, None] * right_weight[None, :] * gauss * cosine
        second_order = first_order * cosine
        pull = -2.0 * factor / width_square
        left_pos_grad = pull * (
            left_pos * jnp.sum(second_order, axis=1)[None, :]
            - jnp.einsum("kb,ab->ka", right_pos, second_order, precision=highest)
        )
        right_pos_grad = pull * (
            right_pos * jnp.sum(second_order, axis=0)[None, :]
            - jnp.einsum("ka,ab->kb", left_pos, second_order, precision=highest)
        )
        left_dir_grad = (
            2.0 * factor * jnp.einsum("kb,ab->ka", right_dir, first_order, precision=highest)
        )
        right_dir_grad = (
            2.0 * factor * jnp.einsum("ka,ab->kb", left_dir, first_order, precision=highest)
        )
        left_parts.append(jnp.concatenate([left_pos_grad, left_dir_grad], axis=0))
        right_grad = right_grad + jnp.concatenate([right_pos_grad, right_dir_grad], axis=0)
    return (jnp.concatenate(left_parts, axis=1), right_grad)


def per_device(centres, tangents, weights, segment_count, pairs, pair_count):
    blocks = centres.shape[1]
    segments = centres.shape[3]
    slot_total = pairs.shape[1]
    loss_scale = segments ** (-0.5)
    live_segment = jnp.arange(segments)[None, :] < segment_count[0][:, None]
    masked = jnp.where(live_segment, weights[0], jnp.zeros_like(weights[0]))
    own_data = jnp.concatenate([centres[0], tangents[0], masked[:, None, :]], axis=1)
    upper_data = from_behind(own_data, "slab", -1)
    window = with_halo(jnp.stack([own_data, upper_data]), (("cells", 1),), REACH)
    extent = blocks + 2 * REACH
    stacked = window.reshape(2 * extent, 7, segments)
    slab_blocks = blocks * lax.axis_size("cells")
    anchor = lax.axis_index("cells") * blocks - REACH
    first = pairs[0, :, 0]
    second = pairs[0, :, 1]
    left_row = first - anchor
    right_row = jnp.where(
        second >= slab_blocks, extent + second - slab_blocks - anchor, second - anchor
    )
    factor = loss_scale * jnp.where(first == second, 1.0, 2.0)
    live_pairs = pair_count[0, 0]

    def one_pair(slot_index, totals, weight_factor):
        left_block = lax.dynamic_index_in_dim(stacked, left_row[slot_index], 0, keepdims=False)
        right_block = lax.dynamic_index_in_dim(stacked, right_row[slot_index], 0, keepdims=False)
        left_grad, right_grad = tile_terms(left_block, right_block, weight_factor[slot_index])
        totals = totals.at[left_row[slot_index]].add(left_grad)
        totals = totals.at[right_row[slot_index]].add(right_grad)
        return totals

    empty = jnp.zeros((2 * extent, 6, segments), jnp.float32)
    gated = factor * (jnp.arange(slot_total) < live_pairs).astype(jnp.float32)
    totals = lax.fori_loop(
        0, slot_total, lambda slot_index, totals: one_pair(slot_index, totals, gated), empty
    )
    contrib = totals.reshape(2, extent, 6, segments)
    with_rims = with_halo(contrib, (("cells", 1),), REACH)
    own_sums = with_rims[:, 2 * REACH : 2 * REACH + blocks]
    own_sums = own_sums.at[:, 0:REACH].add(with_rims[:, 0:REACH])
    own_sums = own_sums.at[:, blocks - REACH : blocks].add(
        with_rims[:, extent + REACH : extent + 2 * REACH]
    )
    from_below = from_behind(own_sums[1], "slab", 1)
    grads = own_sums[0] + from_below
    return (grads[None, :, 0:3], grads[None, :, 3:6])


def solution(mesh):
    placed = (
        P("slab", "cells", None, None),
        P("slab", "cells", None, None),
        P("slab", "cells", None),
        P("slab", "cells"),
        P("slab", "cells", None),
        P("slab", "cells"),
    )
    return jax.shard_map(
        per_device,
        mesh=mesh,
        in_specs=placed,
        out_specs=(P("slab", "cells", None, None), P("slab", "cells", None, None)),
        check_vma=False,
    )
```

profile of v0, /device:TPU:253, one launch (start us, length us, event | category | flops | bytes accessed | tf_op | source)
XLA Modules:
  0.0 323.8 jit_solution(8439599715917932774)
XLA Ops:
  8.3 5.8 %collective-permute-start.1 = (f32[2,2,7,1024]{3,1,2,0:T(2,128)S(1)}, f32[2,2,7,1024]{3,1,2,0:T(2,128)S(1)}, u32[]{:S(2)}, u32[]{:S(2)}) collective-permute-start(f32[2,2,7,1024]{3,1,2,0:T(2,128)S(1)} %get-tuple-element.269), channel_id=1, source_target_pairs={{0,4},{4,8},{8,12},{12,16},{16,20},{20,24},{24,28},{28,32},{32,36}... | collective-permute-start | bytes 344072 | tf_op jit(solution)/shard_map/ppermute | solution.py:23
  16.9 6.7 %collective-permute-done.2 = f32[2,2,7,1024]{3,1,2,0:T(2,128)S(1)} collective-permute-done((f32[2,2,7,1024]{3,1,2,0:T(2,128)S(1)}, f32[2,2,7,1024]{3,1,2,0:T(2,128)S(1)}, u32[]{:S(2)}, u32[]{:S(2)}) %collective-permute-start.2) | collective-permute-done | bytes 114720 | tf_op jit(solution)/shard_map/ppermute | solution.py:26
  24.1 282.0 %while.19 = (s32[]{:T(128)}, f32[16,6,1024]{2,1,0:T(8,128)S(1)}, s32[10]{0:T(128)S(1)}, f32[10]{0:T(128)S(1)}, f32[16,7,1024]{2,1,0:T(8,128)S(1)}, /*index=5*/s3...) while((s32[]{:T(128)}, f32[16,6,1024]{2,1,0:T(8,128)S(1)}, ...), condition=%wide.region_9.10_spmd, body=%wide.region_0.9_spmd.sunk | while | flops 173110320 | bytes 34247100 | solution.py:107
  29.4 3.1 multiply_reduce_fusion.3
  32.6 4.0 %fusion.87 = (f32[1024]{0:T(1024)S(1)}, f32[512]{0:T(512)S(1)}, f32[512,1024]{1,0:T(8,128)S(1)}, f32[512,1024]{1,0:T(8,128)S(1)}, f32[512]{0:T(512)S(1)}, /*inde...) fusion(f32[1024]{0:T(1024)S(1)} %bitcast.161, f32[512]{0:T(512)S(1)} %bitcast.169, ...), kind=kLoop, calls=%fused_computation.75.clone.1 | loop fusion | flops 13628416 | bytes 12627968 | tf_op jit(solution)/shard_map/while/body/eval_jaxpr/reduce_sum | solution.py:60
  57.6 3.1 multiply_reduce_fusion.3
  60.8 4.0 %fusion.87 = (f32[1024]{0:T(1024)S(1)}, f32[512]{0:T(512)S(1)}, f32[512,1024]{1,0:T(8,128)S(1)}, f32[512,1024]{1,0:T(8,128)S(1)}, f32[512]{0:T(512)S(1)}, /*inde...) fusion(f32[1024]{0:T(1024)S(1)} %bitcast.161, f32[512]{0:T(512)S(1)} %bitcast.169, ...), kind=kLoop, calls=%fused_computation.75.clone.1 | loop fusion | flops 13628416 | bytes 12627968 | tf_op jit(solution)/shard_map/while/body/eval_jaxpr/reduce_sum | solution.py:60
  85.8 3.1 multiply_reduce_fusion.3
  89.0 4.0 %fusion.87 = (f32[1024]{0:T(1024)S(1)}, f32[512]{0:T(512)S(1)}, f32[512,1024]{1,0:T(8,128)S(1)}, f32[512,1024]{1,0:T(8,128)S(1)}, f32[512]{0:T(512)S(1)}, /*inde...) fusion(f32[1024]{0:T(1024)S(1)} %bitcast.161, f32[512]{0:T(512)S(1)} %bitcast.169, ...), kind=kLoop, calls=%fused_computation.75.clone.1 | loop fusion | flops 13628416 | bytes 12627968 | tf_op jit(solution)/shard_map/while/body/eval_jaxpr/reduce_sum | solution.py:60
  114.0 3.1 multiply_reduce_fusion.3
  117.2 4.0 %fusion.87 = (f32[1024]{0:T(1024)S(1)}, f32[512]{0:T(512)S(1)}, f32[512,1024]{1,0:T(8,128)S(1)}, f32[512,1024]{1,0:T(8,128)S(1)}, f32[512]{0:T(512)S(1)}, /*inde...) fusion(f32[1024]{0:T(1024)S(1)} %bitcast.161, f32[512]{0:T(512)S(1)} %bitcast.169, ...), kind=kLoop, calls=%fused_computation.75.clone.1 | loop fusion | flops 13628416 | bytes 12627968 | tf_op jit(solution)/shard_map/while/body/eval_jaxpr/reduce_sum | solution.py:60
  142.2 3.1 multiply_reduce_fusion.3
  145.4 4.0 %fusion.87 = (f32[1024]{0:T(1024)S(1)}, f32[512]{0:T(512)S(1)}, f32[512,1024]{1,0:T(8,128)S(1)}, f32[512,1024]{1,0:T(8,128)S(1)}, f32[512]{0:T(512)S(1)}, /*inde...) fusion(f32[1024]{0:T(1024)S(1)} %bitcast.161, f32[512]{0:T(512)S(1)} %bitcast.169, ...), kind=kLoop, calls=%fused_computation.75.clone.1 | loop fusion | flops 13628416 | bytes 12627968 | tf_op jit(solution)/shard_map/while/body/eval_jaxpr/reduce_sum | solution.py:60
  170.4 3.1 multiply_reduce_fusion.3
  173.6 4.0 %fusion.87 = (f32[1024]{0:T(1024)S(1)}, f32[512]{0:T(512)S(1)}, f32[512,1024]{1,0:T(8,128)S(1)}, f32[512,1024]{1,0:T(8,128)S(1)}, f32[512]{0:T(512)S(1)}, /*inde...) fusion(f32[1024]{0:T(1024)S(1)} %bitcast.161, f32[512]{0:T(512)S(1)} %bitcast.169, ...), kind=kLoop, calls=%fused_computation.75.clone.1 | loop fusion | flops 13628416 | bytes 12627968 | tf_op jit(solution)/shard_map/while/body/eval_jaxpr/reduce_sum | solution.py:60
  198.6 3.1 multiply_reduce_fusion.3
  201.8 4.0 %fusion.87 = (f32[1024]{0:T(1024)S(1)}, f32[512]{0:T(512)S(1)}, f32[512,1024]{1,0:T(8,128)S(1)}, f32[512,1024]{1,0:T(8,128)S(1)}, f32[512]{0:T(512)S(1)}, /*inde...) fusion(f32[1024]{0:T(1024)S(1)} %bitcast.161, f32[512]{0:T(512)S(1)} %bitcast.169, ...), kind=kLoop, calls=%fused_computation.75.clone.1 | loop fusion | flops 13628416 | bytes 12627968 | tf_op jit(solution)/shard_map/while/body/eval_jaxpr/reduce_sum | solution.py:60
  226.8 3.1 multiply_reduce_fusion.3
  230.0 4.0 %fusion.87 = (f32[1024]{0:T(1024)S(1)}, f32[512]{0:T(512)S(1)}, f32[512,1024]{1,0:T(8,128)S(1)}, f32[512,1024]{1,0:T(8,128)S(1)}, f32[512]{0:T(512)S(1)}, /*inde...) fusion(f32[1024]{0:T(1024)S(1)} %bitcast.161, f32[512]{0:T(512)S(1)} %bitcast.169, ...), kind=kLoop, calls=%fused_computation.75.clone.1 | loop fusion | flops 13628416 | bytes 12627968 | tf_op jit(solution)/shard_map/while/body/eval_jaxpr/reduce_sum | solution.py:60
  258.2 4.0 %fusion.87 = (f32[1024]{0:T(1024)S(1)}, f32[512]{0:T(512)S(1)}, f32[512,1024]{1,0:T(8,128)S(1)}, f32[512,1024]{1,0:T(8,128)S(1)}, f32[512]{0:T(512)S(1)}, /*inde...) fusion(f32[1024]{0:T(1024)S(1)} %bitcast.161, f32[512]{0:T(512)S(1)} %bitcast.169, ...), kind=kLoop, calls=%fused_computation.75.clone.1 | loop fusion | flops 13628416 | bytes 12627968 | tf_op jit(solution)/shard_map/while/body/eval_jaxpr/reduce_sum | solution.py:60
  283.2 3.1 multiply_reduce_fusion.3
  286.4 4.0 %fusion.87 = (f32[1024]{0:T(1024)S(1)}, f32[512]{0:T(512)S(1)}, f32[512,1024]{1,0:T(8,128)S(1)}, f32[512,1024]{1,0:T(8,128)S(1)}, f32[512]{0:T(512)S(1)}, /*inde...) fusion(f32[1024]{0:T(1024)S(1)} %bitcast.161, f32[512]{0:T(512)S(1)} %bitcast.169, ...), kind=kLoop, calls=%fused_computation.75.clone.1 | loop fusion | flops 13628416 | bytes 12627968 | tf_op jit(solution)/shard_map/while/body/eval_jaxpr/reduce_sum | solution.py:60
  310.9 6.7 %collective-permute-done.4 = f32[2,2,6,1024]{3,1,0,2:T(2,128)S(1)} collective-permute-done((f32[2,2,6,1024]{3,1,0,2:T(2,128)S(1)}, f32[2,2,6,1024]{3,1,0,2:T(2,128)S(1)}, u32[]{:S(2)}, u32[]{:S(2)}) %collective-permute-start.4) | collective-permute-done | bytes 98336 | tf_op jit(solution)/shard_map/ppermute | solution.py:26
  319.7 3.4 %collective-permute-done.5 = f32[4,6,1024]{2,0,1:T(4,128)S(1)} collective-permute-done((f32[4,6,1024]{2,0,1:T(4,128)S(1)}, f32[4,6,1024]{2,0,1:T(4,128)S(1)}, u32[]{:S(2)}, u32[]{:S(2)}) %collective-permute-start.5) | collective-permute-done | bytes 98336 | tf_op jit(solution)/shard_map/ppermute | solution.py:15
  (217 shorter events, 179.1 us)
Async XLA Ops:
  0.6 23.5 %copy-start = (s32[3]{0:T(128)S(1)}, s32[3]{0:T(128)}, u32[]{:S(2)}) copy-start(s32[3]{0:T(128)} %constant.252.clone.1) | copy-start | bytes 40
  2.3 5.9 %collective-permute-start = (f32[4,7,1024]{2,0,1:T(4,128)S(1)}, f32[4,7,1024]{2,0,1:T(4,128)S(1)}, u32[]{:S(2)}, u32[]{:S(2)}) collective-permute-start(f32[4,7,1024]{2,0,1:T(4,128)S(1)} %get-tuple-element.272), channel_id=1, source_target_pairs={{1,0},{2,1},{3,2},{5,4},{6,5},{7,6},{9,8},{10,9},{11,10},{13,12},{... | collective-permute-start | bytes 344072 | tf_op jit(solution)/shard_map/ppermute | solution.py:15
  8.3 8.5 %collective-permute-start.1 = (f32[2,2,7,1024]{3,1,2,0:T(2,128)S(1)}, f32[2,2,7,1024]{3,1,2,0:T(2,128)S(1)}, u32[]{:S(2)}, u32[]{:S(2)}) collective-permute-start(f32[2,2,7,1024]{3,1,2,0:T(2,128)S(1)} %get-tuple-element.269), channel_id=1, source_target_pairs={{0,4},{4,8},{8,12},{12,16},{16,20},{20,24},{24,28},{28,32},{32,36}... | collective-permute-start | bytes 344072 | tf_op jit(solution)/shard_map/ppermute | solution.py:23
  14.2 9.4 %collective-permute-start.2 = (f32[2,2,7,1024]{3,1,2,0:T(2,128)S(1)}, f32[2,2,7,1024]{3,1,2,0:T(2,128)S(1)}, u32[]{:S(2)}, u32[]{:S(2)}) collective-permute-start(f32[2,2,7,1024]{3,1,2,0:T(2,128)S(1)} %get-tuple-element.270), channel_id=1, source_target_pairs={{4,0},{8,4},{12,8},{16,12},{20,16},{24,20},{28,24},{32,28},{36,32}... | collective-permute-start | bytes 344072 | tf_op jit(solution)/shard_map/ppermute | solution.py:26
  306.4 4.4 %collective-permute-start.3 = (f32[2,2,6,1024]{3,1,0,2:T(2,128)S(1)}, f32[2,2,6,1024]{3,1,0,2:T(2,128)S(1)}, u32[]{:S(2)}, u32[]{:S(2)}) collective-permute-start(f32[2,2,6,1024]{3,1,0,2:T(2,128)S(1)} %get-tuple-element.268), channel_id=1, source_target_pairs={{0,4},{4,8},{8,12},{12,16},{16,20},{20,24},{24,28},{28,32},{32,36}... | collective-permute-start | bytes 294920 | tf_op jit(solution)/shard_map/ppermute | solution.py:23
  308.4 9.3 %collective-permute-start.4 = (f32[2,2,6,1024]{3,1,0,2:T(2,128)S(1)}, f32[2,2,6,1024]{3,1,0,2:T(2,128)S(1)}, u32[]{:S(2)}, u32[]{:S(2)}) collective-permute-start(f32[2,2,6,1024]{3,1,0,2:T(2,128)S(1)} %get-tuple-element.267), channel_id=1, source_target_pairs={{4,0},{8,4},{12,8},{16,12},{20,16},{24,20},{28,24},{32,28},{36,32}... | collective-permute-start | bytes 294920 | tf_op jit(solution)/shard_map/ppermute | solution.py:26
  317.8 5.4 %collective-permute-start.5 = (f32[4,6,1024]{2,0,1:T(4,128)S(1)}, f32[4,6,1024]{2,0,1:T(4,128)S(1)}, u32[]{:S(2)}, u32[]{:S(2)}) collective-permute-start(f32[4,6,1024]{2,0,1:T(4,128)S(1)} %slice_bitcast_fusion), channel_id=1, source_target_pairs={{0,1},{1,2},{2,3},{4,5},{5,6},{6,7},{8,9},{9,10},{10,11},{12,13},{... | collective-permute-start | bytes 294920 | tf_op jit(solution)/shard_map/ppermute | solution.py:15
where the time goes:
time: 325 us; the launch traced here: 324 us
  matrix products  118 us (36%)
  other arithmetic  96.5 us (30%)
  loops' own time  52.4 us (16%)
  local copies, waits for them, and re-layouts  20.4 us (6%)
  waiting for transfers between devices  19.2 us (6%)
  starting transfers between devices  16.2 us (5%)
    another operation x1, loops' own time, per_device(): lax.fori_loop(0, slot_total, lambda slot_index, totals: one_pair(slot_ind...  52.4 us
    reduce_sum x10, other arithmetic, tile_terms(): jnp.sum(second_order, axis=0)[None, :]  40.4 us
    dot_general x20, matrix products, tile_terms(): jnp.einsum('kb,ab->ka', right_dir, first_order, precision=highest)  37 us
    dot_general x20, matrix products, tile_terms(): jnp.einsum('kb,ab->ka', right_pos, second_order, precision=highest)  36.7 us
    reduce_sum x10, other arithmetic, tile_terms(): jnp.sum((left_pos[:, :, None] - right_pos[:, None, :]) ** 2, axis=0)  30.8 us
    dot_general x20, matrix products, tile_terms(): jnp.einsum('ka,ab->kb', left_pos, second_order, precision=highest)  22 us
    dot_general x20, matrix products, tile_terms(): jnp.einsum('ka,ab->kb', left_dir, first_order, precision=highest)  22 us
    ppermute x2, waiting for transfers between devices, with_halo(): lax.ppermute(lax.slice_in_dim(block, 0, width, axis=dim), axis, backward)  13.5 us
  transfers between devices with their start and end apart: 6, of which 4 were waited for; matrix products, arithmetic and copies ran while one was open for 1% of the time, Pallas kernels for 0%

commit v1 on v0

v1 whole, which is shorter than its diff:
```python
import functools
import math

import jax
import jax.numpy as jnp
from jax import lax
from jax.experimental import pallas as pl
from jax.experimental.pallas import tpu as pltpu
from jax.sharding import PartitionSpec as P

REACH = 2
WIDTH_SQUARE = 4.0
SCALE = math.sqrt(2.0 * math.log2(math.e) / WIDTH_SQUARE)
F32, BF16 = jnp.float32, jnp.bfloat16
MESH = pl.DeviceIdType.MESH
TILE = 256
MOVES = [(ds, dc) for ds in (0, -1, 1) for dc in (0, -1, 1) if (ds, dc) != (0, 0)]


def region(level, side, blocks):
    extent = blocks + 2 * REACH
    first = (level + 1) * extent
    if side < 0:
        return first, REACH
    if side > 0:
        return first + REACH + blocks, REACH
    return first + REACH, blocks


def gather_kernel(blocks, slots, cen, tan, wts, cnt, prs, pcn, win, meta, send_sem, recv_sem):
    cells, slabs = lax.axis_size("cells"), lax.axis_size("slab")
    c, s = lax.axis_index("cells"), lax.axis_index("slab")
    segments = win.shape[2]
    peers = [
        {"slab": lax.rem(s + ds + slabs, slabs), "cells": lax.rem(c + dc + cells, cells)}
        for ds, dc in MOVES
    ]
    barrier = pltpu.get_barrier_semaphore()
    for peer in peers:
        pl.semaphore_signal(barrier, inc=1, device_id=peer, device_id_type=MESH)
    extent = blocks + 2 * REACH
    own = extent + REACH
    lane = lax.broadcasted_iota(jnp.int32, (1, segments), 1)
    table = jnp.zeros((1, segments), jnp.int32)
    for k in range(slots):
        table = jnp.where(lane == k, prs[0, k, 0], table)
        table = jnp.where(lane == slots + k, prs[0, k, 1], table)
    table = jnp.where(lane == 2 * slots, pcn[0, 0], table)
    for b in range(blocks):
        win[own + b, 0:3, :] = cen[0, b]
        win[own + b, 3:6, :] = tan[0, b]
        win[own + b, 6:7, :] = jnp.where(lane < cnt[0, b], wts[0, b : b + 1, :], 0.0)
        row = jnp.where(lane == 2 * slots + 1, cnt[0, b], table)
        win[own + b, 7:8, :] = row.astype(F32)
    pl.semaphore_wait(barrier, len(MOVES))
    copies = []
    for n, (ds, dc) in enumerate(MOVES):
        target, count = region(-ds, -dc, blocks)
        source = own + (blocks - REACH if dc > 0 else 0)
        copy = pltpu.make_async_remote_copy(
            src_ref=win.at[pl.ds(source, count)],
            dst_ref=win.at[pl.ds(target, count)],
            send_sem=send_sem.at[n],
            recv_sem=recv_sem.at[n],
            device_id=peers[n],
            device_id_type=MESH,
        )
        copy.start()
        copies.append(copy)
    for copy in copies:
        copy.wait()
    for slot in range(3 * extent):
        meta[slot : slot + 1, :] = win[slot, 7:8, 0:128].astype(jnp.int32)
    meta[3 * extent : 3 * extent + 8, :] = jnp.full((8, 128), c, jnp.int32)


def pieces(value):
    high = value.astype(BF16).astype(F32)
    rest = value - high
    middle = rest.astype(BF16).astype(F32)
    return high, middle, rest - middle


def spread(tile, row):
    return jnp.broadcast_to(tile[row : row + 1], tile.shape)


def position_rows(tile, norm_row, one_row):
    row = lax.broadcasted_iota(jnp.int32, tile.shape, 0)
    x, y, z = [spread(tile, r) * SCALE for r in range(3)]
    norm = -0.5 * (x * x + y * y + z * z)
    base = jnp.where(row < 3, tile * SCALE, 0.0)
    return jnp.where(row == norm_row, norm, jnp.where(row == one_row, 1.0, base))


def tangent_products(tile):
    row = lax.broadcasted_iota(jnp.int32, tile.shape, 0)
    t0, t1, t2 = [spread(tile, r) for r in range(3, 6)]
    left = jnp.where(row < 3, t0, jnp.where(row < 5, t1, t2))
    right = jnp.where(row == 0, t0, jnp.where((row == 1) | (row == 3), t1, t2))
    return left * right, row


def prepare_own(win, slot, vr, p):
    p1, p2, p3 = pieces(position_rows(win[slot], 4, 3))
    vr[p] = jnp.concatenate([p1, p2, p1, p2, p3, p1, p3, p2], axis=0).astype(BF16)


def prepare_unit(win, slot, start, ut, ft):
    tile = win[slot, :, pl.ds(start, TILE)]
    q1, q2, q3 = pieces(position_rows(tile, 3, 4))
    ut[...] = jnp.concatenate([q1, q1, q2, q2, q1, q3, q2, q3], axis=0).T.astype(BF16)
    products, row = tangent_products(tile)
    base = jnp.where(row < 6, spread(tile, 6) * products, 0.0)
    terms = jnp.concatenate([base] + [base * spread(tile, k) for k in range(3)], axis=0)
    ft[...] = jnp.concatenate(pieces(terms), axis=0).astype(BF16)


def dot(a, b):
    return lax.dot_general(a, b, (((1,), (0,)), ((), ())), preferred_element_type=F32)


def gauss_step(ut, vr, p, high, low, cols):
    gauss = jnp.exp2(dot(ut[...], vr[p, :, cols]))
    top = gauss.astype(BF16)
    high[:, cols] = top
    low[:, cols] = (gauss - top.astype(F32)).astype(BF16)


def sum_step(ft, high, low, acc, p, cols):
    whole = dot(ft[...], high[:, cols])
    part = dot(ft[0:32], low[:, cols])
    acc[p, :, cols] += whole[0:32] + whole[32:64] + whole[64:96] + part


def pair_kernel(
    blocks, slots, meta, win, gc, gt, acc, vr, ut0, ut1, f0, f1, h0, h1, l0, l1, units, counts
):
    segments = win.shape[2]
    extent = blocks + 2 * REACH
    own = extent + REACH
    chunks = segments // TILE
    cells = lax.axis_size("cells")
    slab_blocks = blocks * cells
    c = meta[3 * extent, 0]
    anchor = c * blocks - REACH
    low_own = c * blocks

    for p in range(blocks):
        counts[p] = 0

    def append(p, slot):
        at = counts[p]
        live = lax.div(meta[slot, 2 * slots + 1] + (TILE - 1), TILE)

        def one(k, carry):
            units[p, at + k] = slot * chunks + k
            return carry

        lax.fori_loop(0, live, one, 0)
        counts[p] = at + live

    def list_source(level, side):
        slot0 = region(level, side, blocks)[0]

        def one(k, carry):
            first = meta[slot0, k]
            second = meta[slot0, slots + k]
            upper = second >= slab_blocks
            if level == 0 and side == 0:
                inside = jnp.where(upper, second - slab_blocks, second)
                append(
                    first - low_own, jnp.where(upper, 2 * extent, extent) + inside - anchor
                )
            target = second - slab_blocks if level < 0 else second
            wanted = (target >= low_own) & (target < low_own + blocks)
            if level == 0:
                wanted = wanted & jnp.logical_not(upper)
            if level == 0 and side == 0:
                wanted = wanted & (first != second)

            @pl.when(wanted)
            def _():
                append(target - low_own, (level + 1) * extent + first - anchor)

            return carry

        lax.fori_loop(0, meta[slot0, 2 * slots], one, 0)

    list_source(0, 0)
    for side in (-1, 1):
        has = c > 0 if side < 0 else c < cells - 1
        pl.when(has)(functools.partial(list_source, 0, side))
        pl.when(has)(functools.partial(list_source, -1, side))
    list_source(-1, 0)

    acc[...] = jnp.zeros_like(acc)
    for p in range(blocks):
        prepare_own(win, own + p, vr, p)

    uts, fts, highs, lows = (ut0, ut1), (f0, f1), (h0, h1), (l0, l1)

    def run(width, p, total):
        step = 512 if width % 512 == 0 else 256

        def place(u):
            unit = units[p, u]
            return lax.div(unit, chunks), pl.multiple_of(lax.rem(unit, chunks) * TILE, TILE)

        def columns(i):
            return slice(i, i + step)

        prepare_unit(win, *place(0), uts[0], fts[0])
        for i in range(0, width, step):
            gauss_step(uts[0], vr, p, highs[0], lows[0], columns(i))
        prepare_unit(win, *place(1), uts[1], fts[1])

        def half(k, u):
            n = 1 - k
            for i in range(0, width, step):
                gauss_step(uts[n], vr, p, highs[n], lows[n], columns(i))
                sum_step(fts[k], highs[k], lows[k], acc, p, columns(i))
            prepare_unit(win, *place(u + 2), uts[k], fts[k])

        def body(m, carry):
            half(0, 2 * m)
            pl.when(2 * m + 1 < total)(functools.partial(half, 1, 2 * m + 1))
            return carry

        lax.fori_loop(0, lax.div(total + 1, 2), body, 0)

    def one_block(p, carry):
        total = counts[p]
        for k in range(2):
            units[p, total + k] = (own + p) * chunks
        width = lax.div(meta[own + p, 2 * slots + 1] + (TILE - 1), TILE)
        for k in range(1, chunks + 1):
            pl.when((width == k) & (total > 0))(functools.partial(run, k * TILE, p, total))
        return carry

    lax.fori_loop(0, blocks, one_block, 0)

    loss_scale = segments**-0.5
    for p in range(blocks):
        tile = win[own + p]
        products, row = tangent_products(tile)
        twice = jnp.where((row == 0) | (row == 3) | (row == 5), 1.0, 2.0)
        forms = jnp.where(row < 6, products * twice, 0.0)
        total = acc[p]
        weight = tile[6:7]
        sums = [
            jnp.sum(forms * total[8 * k : 8 * k + 8], axis=0, keepdims=True) for k in range(4)
        ]
        pull = (-4.0 * loss_scale / WIDTH_SQUARE) * weight
        gc[0, p] = jnp.concatenate(
            [pull * (tile[k : k + 1] * sums[0] - sums[k + 1]) for k in range(3)], axis=0
        )
        m = [total[k : k + 1] for k in range(6)]
        t = [tile[k : k + 1] for k in range(3, 6)]
        turn = (4.0 * loss_scale) * weight
        gt[0, p] = jnp.concatenate(
            [
                turn * (m[0] * t[0] + m[1] * t[1] + m[2] * t[2]),
                turn * (m[1] * t[0] + m[3] * t[1] + m[4] * t[2]),
                turn * (m[2] * t[0] + m[4] * t[1] + m[5] * t[2]),
            ],
            axis=0,
        )


def per_device(centres, tangents, weights, segment_count, pairs, pair_count):
    blocks, segments, slots = centres.shape[1], centres.shape[3], pairs.shape[1]
    extent = blocks + 2 * REACH
    vmem = pl.BlockSpec(memory_space=pltpu.VMEM)
    smem = pl.BlockSpec(memory_space=pltpu.SMEM)
    window, meta = pl.pallas_call(
        functools.partial(gather_kernel, blocks, slots),
        out_shape=(
            jax.ShapeDtypeStruct((3 * extent, 8, segments), F32),
            jax.ShapeDtypeStruct((3 * extent + 8, 128), jnp.int32),
        ),
        in_specs=[vmem, vmem, vmem, smem, smem, smem],
        out_specs=(vmem, vmem),
        scratch_shapes=[
            pltpu.SemaphoreType.DMA((len(MOVES),)),
            pltpu.SemaphoreType.DMA((len(MOVES),)),
        ],
        compiler_params=pltpu.CompilerParams(collective_id=0, has_side_effects=True),
        name="gather_window",
    )(centres, tangents, weights, segment_count, pairs, pair_count)
    most = (2 * REACH + 1) * 3 * (segments // TILE) + 4
    return pl.pallas_call(
        functools.partial(pair_kernel, blocks, slots),
        out_shape=(
            jax.ShapeDtypeStruct((1, blocks, 3, segments), F32),
            jax.ShapeDtypeStruct((1, blocks, 3, segments), F32),
        ),
        in_specs=[smem, vmem],
        out_specs=(vmem, vmem),
        scratch_shapes=[
            pltpu.VMEM((blocks, 32, segments), F32),
            pltpu.VMEM((blocks, 64, segments), BF16),
            pltpu.VMEM((TILE, 64), BF16),
            pltpu.VMEM((TILE, 64), BF16),
            pltpu.VMEM((96, TILE), BF16),
            pltpu.VMEM((96, TILE), BF16),
            pltpu.VMEM((TILE, segments), BF16),
            pltpu.VMEM((TILE, segments), BF16),
            pltpu.VMEM((TILE, segments), BF16),
            pltpu.VMEM((TILE, segments), BF16),
            pltpu.SMEM((blocks, most), jnp.int32),
            pltpu.SMEM((blocks,), jnp.int32),
        ],
        compiler_params=pltpu.CompilerParams(vmem_limit_bytes=32 << 20),
        name="pair_sums",
    )(meta, window)


def solution(mesh):
    placed = (
        P("slab", "cells", None, None),
        P("slab", "cells", None, None),
        P("slab", "cells", None),
        P("slab", "cells"),
        P("slab", "cells", None),
        P("slab", "cells"),
    )
    return jax.shard_map(
        per_device,
        mesh=mesh,
        in_specs=placed,
        out_specs=(P("slab", "cells", None, None), P("slab", "cells", None, None)),
        check_vma=False,
    )
```

time: 325 us -> 51.2 us (0.16)
  the two profiles are of different devices: /device:TPU:253 before, /device:TPU:78 now
where the time goes in v1:
time: 51.2 us; the launch traced here: 50.9 us
  Pallas kernels  43.6 us (85%)
  local copies, waits for them, and re-layouts  5.98 us (12%)
  between operations  1.33 us (3%)
    pallas_call x1, Pallas kernels, per_device(): pl.pallas_call(functools.partial(pair_kernel, blocks, slots), out_shape=(...  30.4 us
    pallas_call x1, Pallas kernels, per_device(): pl.pallas_call(functools.partial(gather_kernel, blocks, slots), out_shape...  13.1 us
    unnamed x11, local copies, waits for them, and re-layouts  4.68 us
    pallas_call x2, local copies, waits for them, and re-layouts, per_device(): pl.pallas_call(functools.partial(pair_kernel, blocks, slots), out_shape=(...  1.31 us

profile of v1, /device:TPU:78, one launch (start us, length us, event | category | flops | bytes accessed | tf_op | source)
XLA Modules:
  0.0 50.9 jit_solution(9703998777901248933)
XLA Ops:
  0.6 0.0 copy-start.3
  1.3 0.0 copy-done.3
  1.3 0.7 %copy.10.prs = s32[1,10,2]{2,1,0:T(8,128)} copy(s32[1,10,2]{1,2,0:T(2,128)S(1)} %copy-done.3) | data formatting | bytes 160 | tf_op args[4]
  2.0 0.0 copy-start.2
  2.0 1.5 %copy.8.cen = f32[1,4,3,1024]{3,2,1,0:T(4,128)} copy(f32[1,4,3,1024]{3,1,2,0:T(4,128)} %param.6) | data formatting | bytes 98304 | tf_op args[0]
  3.5 0.0 copy-done.2
  3.5 0.7 %copy.9.tan = f32[1,4,3,1024]{3,2,1,0:T(4,128)} copy(f32[1,4,3,1024]{3,1,2,0:T(4,128)S(1)} %copy-done.2) | data formatting | bytes 98304 | tf_op args[1]
  4.1 13.1 %gather_window.1 = (f32[24,8,1024]{2,1,0:T(8,128)}, s32[32,128]{1,0:T(8,128)}) custom-call(f32[1,4,3,1024]{3,2,1,0:T(4,128)} %copy.8.cen, f32[1,4,3,1024]{3,2,1,0:T(4,128)} %copy.9.tan, f32[1,4,1024]{2,1,0:T(4,128)} %wts.1, s32[1,4]{1,0:T(1,128)} %cnt.1, s32[1,10,2]{2,1,0:T(8,128)} %copy.10.prs, s32[1,1]{1,0:T(1,128)S(6)} %copy.13.pcn), custom_call_target="tpu_custom_call" | custom-call | tf_op jit(solution)/shard_map/gather_window/pallas_call | solution.py:276
  17.3 0.0 copy-start
  17.3 1.1 %copy-done = f32[24,8,1024]{2,1,0:T(8,128)S(1)} copy-done((f32[24,8,1024]{2,1,0:T(8,128)S(1)}, f32[24,8,1024]{2,1,0:T(8,128)}, u32[]{:S(2)}) %copy-start) | copy-done | bytes 786456
  18.4 0.0 copy-start.1
  18.4 0.7 %copy-done.1 = s32[32,128]{1,0:T(8,128)S(1)} copy-done((s32[32,128]{1,0:T(8,128)S(1)}, s32[32,128]{1,0:T(8,128)}, u32[]{:S(2)}) %copy-start.1) | copy-done | bytes 16408
  19.1 30.4 %pair_sums.1 = (f32[1,4,3,1024]{3,2,1,0:T(4,128)S(1)}, f32[1,4,3,1024]{3,2,1,0:T(4,128)S(1)}) custom-call(s32[32,128]{1,0:T(8,128)S(1)} %copy-done.1, f32[24,8,1024]{2,1,0:T(8,128)S(1)} %copy-done), custom_call_target="tpu_custom_call" | custom-call | tf_op jit(solution)/shard_map/pair_sums/pallas_call | solution.py:292
  49.6 0.7 %copy.11 = f32[1,4,3,1024]{3,1,2,0:T(4,128)} copy(f32[1,4,3,1024]{3,2,1,0:T(4,128)S(1)} %get-tuple-element.6) | data formatting | bytes 98304 | tf_op jit(solution)/shard_map/pair_sums/pallas_call | solution.py:292
  50.2 0.7 %copy.12 = f32[1,4,3,1024]{3,1,2,0:T(4,128)} copy(f32[1,4,3,1024]{3,2,1,0:T(4,128)S(1)} %get-tuple-element.7) | data formatting | bytes 98304 | tf_op jit(solution)/shard_map/pair_sums/pallas_call | solution.py:292
Async XLA Ops:
  0.6 0.7 %copy-start.3 = (s32[1,10,2]{1,2,0:T(2,128)S(1)}, s32[1,10,2]{1,2,0:T(2,128)}, u32[]{:S(2)}) copy-start(s32[1,10,2]{1,2,0:T(2,128)} %param.10) | copy-start | bytes 244
  2.0 1.5 %copy-start.2 = (f32[1,4,3,1024]{3,1,2,0:T(4,128)S(1)}, f32[1,4,3,1024]{3,1,2,0:T(4,128)}, u32[]{:S(2)}) copy-start(f32[1,4,3,1024]{3,1,2,0:T(4,128)} %param.7) | copy-start | bytes 147460
  17.3 1.1 %copy-start = (f32[24,8,1024]{2,1,0:T(8,128)S(1)}, f32[24,8,1024]{2,1,0:T(8,128)}, u32[]{:S(2)}) copy-start(f32[24,8,1024]{2,1,0:T(8,128)} %get-tuple-element.5.win) | copy-start | bytes 2359300
  18.4 0.7 %copy-start.1 = (s32[32,128]{1,0:T(8,128)S(1)}, s32[32,128]{1,0:T(8,128)}, u32[]{:S(2)}) copy-start(s32[32,128]{1,0:T(8,128)} %get-tuple-element.4.meta) | copy-start | bytes 49156

commit v2 on v1

--- a/solution.py
+++ b/solution.py
@@ -43,12 +43,13 @@
     lane = lax.broadcasted_iota(jnp.int32, (1, segments), 1)
     table = jnp.zeros((1, segments), jnp.int32)
     for k in range(slots):
-        table = jnp.where(lane == k, prs[0, k, 0], table)
-        table = jnp.where(lane == slots + k, prs[0, k, 1], table)
+        table = jnp.where(lane == k, prs[0, k], table)
+        table = jnp.where(lane == slots + k, prs[1, k], table)
     table = jnp.where(lane == 2 * slots, pcn[0, 0], table)
     for b in range(blocks):
-        win[own + b, 0:3, :] = cen[0, b]
-        win[own + b, 3:6, :] = tan[0, b]
+        for k in range(3):
+            win[own + b, k : k + 1, :] = cen[k, b : b + 1, :]
+            win[own + b, 3 + k : 4 + k, :] = tan[k, b : b + 1, :]
         win[own + b, 6:7, :] = jnp.where(lane < cnt[0, b], wts[0, b : b + 1, :], 0.0)
         row = jnp.where(lane == 2 * slots + 1, cnt[0, b], table)
         win[own + b, 7:8, :] = row.astype(F32)
@@ -134,8 +135,15 @@
 
 
 def pair_kernel(
-    blocks, slots, meta, win, gc, gt, acc, vr, ut0, ut1, f0, f1, h0, h1, l0, l1, units, counts
+    blocks, slots, meta_hbm, win_hbm, gc, gt, win, acc, vr, ut0, ut1, f0, f1, h0, h1, l0, l1,
+    meta, units, counts, sems,
 ):
+    table_copy = pltpu.make_async_copy(meta_hbm, meta, sems.at[0])
+    window_copy = pltpu.make_async_copy(win_hbm, win, sems.at[1])
+    table_copy.start()
+    window_copy.start()
+    acc[...] = jnp.zeros_like(acc)
+    table_copy.wait()
     segments = win.shape[2]
     extent = blocks + 2 * REACH
     own = extent + REACH
@@ -194,7 +202,7 @@
         pl.when(has)(functools.partial(list_source, -1, side))
     list_source(-1, 0)
 
-    acc[...] = jnp.zeros_like(acc)
+    window_copy.wait()
     for p in range(blocks):
         prepare_own(win, own + p, vr, p)
 
@@ -252,20 +260,13 @@
             jnp.sum(forms * total[8 * k : 8 * k + 8], axis=0, keepdims=True) for k in range(4)
         ]
         pull = (-4.0 * loss_scale / WIDTH_SQUARE) * weight
-        gc[0, p] = jnp.concatenate(
-            [pull * (tile[k : k + 1] * sums[0] - sums[k + 1]) for k in range(3)], axis=0
-        )
+        for k in range(3):
+            gc[k, p : p + 1, :] = pull * (tile[k : k + 1] * sums[0] - sums[k + 1])
         m = [total[k : k + 1] for k in range(6)]
         t = [tile[k : k + 1] for k in range(3, 6)]
         turn = (4.0 * loss_scale) * weight
-        gt[0, p] = jnp.concatenate(
-            [
-                turn * (m[0] * t[0] + m[1] * t[1] + m[2] * t[2]),
-                turn * (m[1] * t[0] + m[3] * t[1] + m[4] * t[2]),
-                turn * (m[2] * t[0] + m[4] * t[1] + m[5] * t[2]),
-            ],
-            axis=0,
-        )
+        for k, (x, y, z) in enumerate(((0, 1, 2), (1, 3, 4), (2, 4, 5))):
+            gt[k, p : p + 1, :] = turn * (m[x] * t[0] + m[y] * t[1] + m[z] * t[2])
 
 
 def per_device(centres, tangents, weights, segment_count, pairs, pair_count):
@@ -287,17 +288,26 @@
         ],
         compiler_params=pltpu.CompilerParams(collective_id=0, has_side_effects=True),
         name="gather_window",
-    )(centres, tangents, weights, segment_count, pairs, pair_count)
+    )(
+        jnp.transpose(centres[0], (1, 0, 2)),
+        jnp.transpose(tangents[0], (1, 0, 2)),
+        weights,
+        segment_count,
+        jnp.transpose(pairs[0]),
+        pair_count,
+    )
     most = (2 * REACH + 1) * 3 * (segments // TILE) + 4
-    return pl.pallas_call(
+    hbm = pl.BlockSpec(memory_space=pltpu.HBM)
+    grads = pl.pallas_call(
         functools.partial(pair_kernel, blocks, slots),
         out_shape=(
-            jax.ShapeDtypeStruct((1, blocks, 3, segments), F32),
-            jax.ShapeDtypeStruct((1, blocks, 3, segments), F32),
+            jax.ShapeDtypeStruct((3, blocks, segments), F32),
+            jax.ShapeDtypeStruct((3, blocks, segments), F32),
         ),
-        in_specs=[smem, vmem],
+        in_specs=[hbm, hbm],
         out_specs=(vmem, vmem),
         scratch_shapes=[
+            pltpu.VMEM((3 * extent, 8, segments), F32),
             pltpu.VMEM((blocks, 32, segments), F32),
             pltpu.VMEM((blocks, 64, segments), BF16),
             pltpu.VMEM((TILE, 64), BF16),
@@ -308,12 +318,15 @@
             pltpu.VMEM((TILE, segments), BF16),
             pltpu.VMEM((TILE, segments), BF16),
             pltpu.VMEM((TILE, segments), BF16),
+            pltpu.SMEM((3 * extent + 8, 128), jnp.int32),
             pltpu.SMEM((blocks, most), jnp.int32),
             pltpu.SMEM((blocks,), jnp.int32),
+            pltpu.SemaphoreType.DMA((2,)),
         ],
-        compiler_params=pltpu.CompilerParams(vmem_limit_bytes=32 << 20),
+        compiler_params=pltpu.CompilerParams(vmem_limit_bytes=60 << 20),
         name="pair_sums",
     )(meta, window)
+    return tuple(jnp.transpose(grad, (1, 0, 2))[None] for grad in grads)
 
 
 def solution(mesh):

time: 51.2 us -> 42.7 us (0.83)
  the two profiles are of different devices: /device:TPU:78 before, /device:TPU:2 now
where the time goes in v2:
time: 42.7 us; the launch traced here: 42.5 us
  Pallas kernels  41.2 us (96%)
  between operations  1.29 us (3%)
    pallas_call x1, Pallas kernels, per_device(): pl.pallas_call(functools.partial(pair_kernel, blocks, slots), out_shape=(...  20.7 us
    pallas_call x1, Pallas kernels, per_device(): pl.pallas_call(functools.partial(gather_kernel, blocks, slots), out_shape...  20.5 us

profile of v2, /device:TPU:2, one launch (start us, length us, event | category | flops | bytes accessed | tf_op | source)
XLA Modules:
  0.0 42.5 jit_solution(1227671807475069244)
XLA Ops:
  1.3 20.5 %gather_window.1 = (f32[24,8,1024]{2,1,0:T(8,128)}, s32[32,128]{1,0:T(8,128)}) custom-call(f32[3,4,1024]{2,1,0:T(4,128)} %bitcast.15, f32[3,4,1024]{2,1,0:T(4,128)} %bitcast.16, f32[1,4,1024]{2,1,0:T(4,128)} %wts.1, s32[1,4]{1,0:T(1,128)} %cnt.1, s32[2,10]{1,0:T(2,128)} %bitcast.17, s32[1,1]{1,0:T(1,128)S(6)} %copy.8.pcn), custom_call_target="tpu_custom_call" | custom-call | tf_op jit(solution)/shard_map/gather_window/pallas_call | solution.py:277
  21.8 20.7 %pair_sums.1 = (f32[3,4,1024]{2,1,0:T(4,128)}, f32[3,4,1024]{2,1,0:T(4,128)}) custom-call(s32[32,128]{1,0:T(8,128)} %get-tuple-element.6.meta_hbm, f32[24,8,1024]{2,1,0:T(8,128)} %get-tuple-element.7.win_hbm), custom_call_target="tpu_custom_call" | custom-call | tf_op jit(solution)/shard_map/pair_sums/pallas_call | solution.py:301

commit v3 on v2

--- a/solution.py
+++ b/solution.py
@@ -13,7 +13,9 @@
 SCALE = math.sqrt(2.0 * math.log2(math.e) / WIDTH_SQUARE)
 F32, BF16 = jnp.float32, jnp.bfloat16
 MESH = pl.DeviceIdType.MESH
-TILE = 256
+TILE = 128
+GROUP = 4
+STRIP = 256
 MOVES = [(ds, dc) for ds in (0, -1, 1) for dc in (0, -1, 1) if (ds, dc) != (0, 0)]
 
 
@@ -107,8 +109,8 @@
     vr[p] = jnp.concatenate([p1, p2, p1, p2, p3, p1, p3, p2], axis=0).astype(BF16)
 
 
-def prepare_unit(win, slot, start, ut, ft):
-    tile = win[slot, :, pl.ds(start, TILE)]
+def prepare_unit(win, places, ut, ft):
+    tile = jnp.concatenate([win[slot, :, pl.ds(start, TILE)] for slot, start in places], axis=1)
     q1, q2, q3 = pieces(position_rows(tile, 3, 4))
     ut[...] = jnp.concatenate([q1, q1, q2, q2, q1, q3, q2, q3], axis=0).T.astype(BF16)
     products, row = tangent_products(tile)
@@ -139,10 +141,13 @@
     meta, units, counts, sems,
 ):
     table_copy = pltpu.make_async_copy(meta_hbm, meta, sems.at[0])
-    window_copy = pltpu.make_async_copy(win_hbm, win, sems.at[1])
+    window_copy = pltpu.make_async_copy(
+        win_hbm, win.at[pl.ds(0, win_hbm.shape[0])], sems.at[1]
+    )
     table_copy.start()
     window_copy.start()
     acc[...] = jnp.zeros_like(acc)
+    win[win_hbm.shape[0]] = jnp.zeros(win.shape[1:], F32)
     table_copy.wait()
     segments = win.shape[2]
     extent = blocks + 2 * REACH
@@ -161,11 +166,8 @@
         at = counts[p]
         live = lax.div(meta[slot, 2 * slots + 1] + (TILE - 1), TILE)
 
-        def one(k, carry):
+        for k in range(chunks):
             units[p, at + k] = slot * chunks + k
-            return carry
-
-        lax.fori_loop(0, live, one, 0)
         counts[p] = at + live
 
     def list_source(level, side):
@@ -209,26 +211,27 @@
     uts, fts, highs, lows = (ut0, ut1), (f0, f1), (h0, h1), (l0, l1)
 
     def run(width, p, total):
-        step = 512 if width % 512 == 0 else 256
-
-        def place(u):
-            unit = units[p, u]
-            return lax.div(unit, chunks), pl.multiple_of(lax.rem(unit, chunks) * TILE, TILE)
-
-        def columns(i):
-            return slice(i, i + step)
-
-        prepare_unit(win, *place(0), uts[0], fts[0])
-        for i in range(0, width, step):
-            gauss_step(uts[0], vr, p, highs[0], lows[0], columns(i))
-        prepare_unit(win, *place(1), uts[1], fts[1])
+        strips = [slice(i, min(i + STRIP, width)) for i in range(0, width, STRIP)]
+
+        def places(u):
+            found = []
+            for k in range(GROUP):
+                unit = units[p, GROUP * u + k]
+                start = pl.multiple_of(lax.rem(unit, chunks) * TILE, TILE)
+                found.append((lax.div(unit, chunks), start))
+            return found
+
+        prepare_unit(win, places(0), uts[0], fts[0])
+        for cols in strips:
+            gauss_step(uts[0], vr, p, highs[0], lows[0], cols)
+        prepare_unit(win, places(1), uts[1], fts[1])
 
         def half(k, u):
             n = 1 - k
-            for i in range(0, width, step):
-                gauss_step(uts[n], vr, p, highs[n], lows[n], columns(i))
-                sum_step(fts[k], highs[k], lows[k], acc, p, columns(i))
-            prepare_unit(win, *place(u + 2), uts[k], fts[k])
+            for cols in strips:
+                sum_step(fts[k], highs[k], lows[k], acc, p, cols)
+                gauss_step(uts[n], vr, p, highs[n], lows[n], cols)
+            prepare_unit(win, places(u + 2), uts[k], fts[k])
 
         def body(m, carry):
             half(0, 2 * m)
@@ -239,11 +242,13 @@
 
     def one_block(p, carry):
         total = counts[p]
-        for k in range(2):
-            units[p, total + k] = (own + p) * chunks
+        for k in range(3 * GROUP):
+            units[p, total + k] = 3 * extent * chunks
         width = lax.div(meta[own + p, 2 * slots + 1] + (TILE - 1), TILE)
-        for k in range(1, chunks + 1):
-            pl.when((width == k) & (total > 0))(functools.partial(run, k * TILE, p, total))
+        for k in range(chunks // 2, chunks + 1):
+            pl.when((width == k) & (total > 0))(
+                functools.partial(run, k * TILE, p, lax.div(total + GROUP - 1, GROUP))
+            )
         return carry
 
     lax.fori_loop(0, blocks, one_block, 0)
@@ -296,7 +301,7 @@
         jnp.transpose(pairs[0]),
         pair_count,
     )
-    most = (2 * REACH + 1) * 3 * (segments // TILE) + 4
+    most = (2 * REACH + 1) * 3 * (segments // TILE) + 3 * GROUP
     hbm = pl.BlockSpec(memory_space=pltpu.HBM)
     grads = pl.pallas_call(
         functools.partial(pair_kernel, blocks, slots),
@@ -307,17 +312,17 @@
         in_specs=[hbm, hbm],
         out_specs=(vmem, vmem),
         scratch_shapes=[
-            pltpu.VMEM((3 * extent, 8, segments), F32),
+            pltpu.VMEM((3 * extent + 1, 8, segments), F32),
             pltpu.VMEM((blocks, 32, segments), F32),
             pltpu.VMEM((blocks, 64, segments), BF16),
-            pltpu.VMEM((TILE, 64), BF16),
-            pltpu.VMEM((TILE, 64), BF16),
-            pltpu.VMEM((96, TILE), BF16),
-            pltpu.VMEM((96, TILE), BF16),
-            pltpu.VMEM((TILE, segments), BF16),
-            pltpu.VMEM((TILE, segments), BF16),
-            pltpu.VMEM((TILE, segments), BF16),
-            pltpu.VMEM((TILE, segments), BF16),
+            pltpu.VMEM((GROUP * TILE, 64), BF16),
+            pltpu.VMEM((GROUP * TILE, 64), BF16),
+            pltpu.VMEM((96, GROUP * TILE), BF16),
+            pltpu.VMEM((96, GROUP * TILE), BF16),
+            pltpu.VMEM((GROUP * TILE, segments), BF16),
+            pltpu.VMEM((GROUP * TILE, segments), BF16),
+            pltpu.VMEM((GROUP * TILE, segments), BF16),
+            pltpu.VMEM((GROUP * TILE, segments), BF16),
             pltpu.SMEM((3 * extent + 8, 128), jnp.int32),
             pltpu.SMEM((blocks, most), jnp.int32),
             pltpu.SMEM((blocks,), jnp.int32),

time: 42.7 us -> 45 us (1.054)
  Pallas kernels: 41.2 us -> 43.5 us
    pallas_call x1, Pallas kernels: 20.7 us -> 23 us  [per_device(): pl.pallas_call(functools.partial(pair_kernel, blocks, slots), out_shape=(...]
where the time goes in v3:
time: 45 us; the launch traced here: 44.8 us
  Pallas kernels  43.5 us (97%)
  between operations  1.29 us (3%)
    pallas_call x1, Pallas kernels, per_device(): pl.pallas_call(functools.partial(pair_kernel, blocks, slots), out_shape=(...  23 us
    pallas_call x1, Pallas kernels, per_device(): pl.pallas_call(functools.partial(gather_kernel, blocks, slots), out_shape...  20.5 us

profile of v3, /device:TPU:2, one launch (start us, length us, event | category | flops | bytes accessed | tf_op | source)
XLA Modules:
  0.0 44.8 jit_solution(13237563145652117400)
XLA Ops:
  1.3 20.5 %gather_window.1 = (f32[24,8,1024]{2,1,0:T(8,128)}, s32[32,128]{1,0:T(8,128)}) custom-call(f32[3,4,1024]{2,1,0:T(4,128)} %bitcast.15, f32[3,4,1024]{2,1,0:T(4,128)} %bitcast.16, f32[1,4,1024]{2,1,0:T(4,128)} %wts.1, s32[1,4]{1,0:T(1,128)} %cnt.1, s32[2,10]{1,0:T(2,128)} %bitcast.17, s32[1,1]{1,0:T(1,128)S(6)} %copy.8.pcn), custom_call_target="tpu_custom_call" | custom-call | tf_op jit(solution)/shard_map/gather_window/pallas_call | solution.py:282
  21.8 23.0 %pair_sums.1 = (f32[3,4,1024]{2,1,0:T(4,128)}, f32[3,4,1024]{2,1,0:T(4,128)}) custom-call(s32[32,128]{1,0:T(8,128)} %get-tuple-element.6.meta_hbm, f32[24,8,1024]{2,1,0:T(8,128)} %get-tuple-element.7.win_hbm), custom_call_target="tpu_custom_call" | custom-call | tf_op jit(solution)/shard_map/pair_sums/pallas_call | solution.py:306

commit v4 on v3

--- a/solution.py
+++ b/solution.py
@@ -16,32 +16,49 @@
 TILE = 128
 GROUP = 4
 STRIP = 256
-MOVES = [(ds, dc) for ds in (0, -1, 1) for dc in (0, -1, 1) if (ds, dc) != (0, 0)]
-
-
-def region(level, side, blocks):
-    extent = blocks + 2 * REACH
-    first = (level + 1) * extent
-    if side < 0:
-        return first, REACH
-    if side > 0:
-        return first + REACH + blocks, REACH
-    return first + REACH, blocks
+SIDES = ((-1, 0), (1, 0), (0, -1), (0, 1))
+
+
+def when(condition, action):
+    pl.when(condition)(action)
 
 
 def gather_kernel(blocks, slots, cen, tan, wts, cnt, prs, pcn, win, meta, send_sem, recv_sem):
     cells, slabs = lax.axis_size("cells"), lax.axis_size("slab")
     c, s = lax.axis_index("cells"), lax.axis_index("slab")
     segments = win.shape[2]
-    peers = [
-        {"slab": lax.rem(s + ds + slabs, slabs), "cells": lax.rem(c + dc + cells, cells)}
-        for ds, dc in MOVES
-    ]
-    barrier = pltpu.get_barrier_semaphore()
-    for peer in peers:
-        pl.semaphore_signal(barrier, inc=1, device_id=peer, device_id_type=MESH)
     extent = blocks + 2 * REACH
     own = extent + REACH
+    there = {(-1, 0): s > 0, (1, 0): s < slabs - 1, (0, -1): c > 0, (0, 1): c < cells - 1}
+
+    def device(ds, dc):
+        return {
+            "slab": lax.rem(s + ds + slabs, slabs),
+            "cells": lax.rem(c + dc + cells, cells),
+        }
+
+    barrier = pltpu.get_barrier_semaphore()
+    for side in SIDES:
+
+        def greet(side=side):
+            pl.semaphore_signal(
+                barrier, inc=1, device_id=device(*side), device_id_type=MESH
+            )
+
+        when(there[side], greet)
+
+    def clear(first, count):
+        def store():
+            win[pl.ds(first, count)] = jnp.zeros((count,) + win.shape[1:], F32)
+
+        return store
+
+    when(s == 0, clear(0, extent))
+    when(s == slabs - 1, clear(2 * extent, extent))
+    for level in range(3):
+        when(c == 0, clear(level * extent, REACH))
+        when(c == cells - 1, clear(level * extent + REACH + blocks, REACH))
+
     lane = lax.broadcasted_iota(jnp.int32, (1, segments), 1)
     table = jnp.zeros((1, segments), jnp.int32)
     for k in range(slots):
@@ -55,23 +72,50 @@
         win[own + b, 6:7, :] = jnp.where(lane < cnt[0, b], wts[0, b : b + 1, :], 0.0)
         row = jnp.where(lane == 2 * slots + 1, cnt[0, b], table)
         win[own + b, 7:8, :] = row.astype(F32)
-    pl.semaphore_wait(barrier, len(MOVES))
-    copies = []
-    for n, (ds, dc) in enumerate(MOVES):
-        target, count = region(-ds, -dc, blocks)
-        source = own + (blocks - REACH if dc > 0 else 0)
-        copy = pltpu.make_async_remote_copy(
+    pl.semaphore_wait(barrier, sum(there[side].astype(jnp.int32) for side in SIDES))
+
+    used = iter(range(send_sem.shape[0]))
+
+    def copy(source, target, count, side):
+        n = next(used)
+        return pltpu.make_async_remote_copy(
             src_ref=win.at[pl.ds(source, count)],
             dst_ref=win.at[pl.ds(target, count)],
             send_sem=send_sem.at[n],
             recv_sem=recv_sem.at[n],
-            device_id=peers[n],
+            device_id=device(*side),
             device_id_type=MESH,
         )
-        copy.start()
-        copies.append(copy)
-    for copy in copies:
-        copy.wait()
+
+    rims = {-1: 0, 1: blocks - REACH}
+    halos = {-1: REACH + blocks, 1: 0}
+    first_hop, second_hop = [], []
+    for ds in (-1, 1):
+        for dc in (-1, 1):
+            block = rims[dc]
+            one = copy(own + block, (1 - ds) * extent + REACH + block, REACH, (ds, 0))
+            when(there[ds, 0], one.start)
+            first_hop.append((ds, dc, one))
+    beside = []
+    for dc in (-1, 1):
+        one = copy(own + rims[dc], extent + halos[dc], REACH, (0, dc))
+        when(there[0, dc], one.start)
+        beside.append((dc, one))
+    for ds, dc, one in first_hop:
+        came = there[-ds, 0]
+        when(came, one.wait_recv)
+        level = (1 - ds) * extent
+        more = copy(level + REACH + rims[dc], level + halos[dc], REACH, (0, dc))
+        when(came & there[0, dc], more.start)
+        second_hop.append((came, dc, more))
+    for ds, dc, one in first_hop:
+        when(there[ds, 0], one.wait_send)
+    for dc, one in beside:
+        when(there[0, dc], one.wait_send)
+        when(there[0, -dc], one.wait_recv)
+    for came, dc, more in second_hop:
+        when(came & there[0, dc], more.wait_send)
+        when(came & there[0, -dc], more.wait_recv)
     for slot in range(3 * extent):
         meta[slot : slot + 1, :] = win[slot, 7:8, 0:128].astype(jnp.int32)
     meta[3 * extent : 3 * extent + 8, :] = jnp.full((8, 128), c, jnp.int32)
@@ -171,7 +215,7 @@
         counts[p] = at + live
 
     def list_source(level, side):
-        slot0 = region(level, side, blocks)[0]
+        slot0 = (level + 1) * extent + {-1: 0, 0: REACH, 1: REACH + blocks}[side]
 
         def one(k, carry):
             first = meta[slot0, k]
@@ -288,8 +332,8 @@
         in_specs=[vmem, vmem, vmem, smem, smem, smem],
         out_specs=(vmem, vmem),
         scratch_shapes=[
-            pltpu.SemaphoreType.DMA((len(MOVES),)),
-            pltpu.SemaphoreType.DMA((len(MOVES),)),
+            pltpu.SemaphoreType.DMA((10,)),
+            pltpu.SemaphoreType.DMA((10,)),
         ],
         compiler_params=pltpu.CompilerParams(collective_id=0, has_side_effects=True),
         name="gather_window",

time: 45 us -> 38.4 us (0.85)
  the two profiles are of different devices: /device:TPU:2 before, /device:TPU:163 now
where the time goes in v4:
time: 38.4 us; the launch traced here: 38.2 us
  Pallas kernels  36.9 us (96%)
  between operations  1.29 us (3%)
    pallas_call x1, Pallas kernels, per_device(): pl.pallas_call(functools.partial(pair_kernel, blocks, slots), out_shape=(...  25.1 us
    pallas_call x1, Pallas kernels, per_device(): pl.pallas_call(functools.partial(gather_kernel, blocks, slots), out_shape...  11.8 us

profile of v4, /device:TPU:163, one launch (start us, length us, event | category | flops | bytes accessed | tf_op | source)
XLA Modules:
  0.0 38.2 jit_solution(7043991210613146653)
XLA Ops:
  1.3 11.8 %gather_window.1 = (f32[24,8,1024]{2,1,0:T(8,128)}, s32[32,128]{1,0:T(8,128)}) custom-call(f32[3,4,1024]{2,1,0:T(4,128)} %bitcast.15, f32[3,4,1024]{2,1,0:T(4,128)} %bitcast.16, f32[1,4,1024]{2,1,0:T(4,128)} %wts.1, s32[1,4]{1,0:T(1,128)} %cnt.1, s32[2,10]{1,0:T(2,128)} %bitcast.17, s32[1,1]{1,0:T(1,128)S(6)} %copy.8.pcn), custom_call_target="tpu_custom_call" | custom-call | tf_op jit(solution)/shard_map/gather_window/pallas_call | solution.py:326
  13.1 25.1 %pair_sums.1 = (f32[3,4,1024]{2,1,0:T(4,128)}, f32[3,4,1024]{2,1,0:T(4,128)}) custom-call(s32[32,128]{1,0:T(8,128)} %get-tuple-element.6.meta_hbm, f32[24,8,1024]{2,1,0:T(8,128)} %get-tuple-element.7.win_hbm), custom_call_target="tpu_custom_call" | custom-call | tf_op jit(solution)/shard_map/pair_sums/pallas_call | solution.py:350
